TPU v7x, 32 devices: a whole 2x2x4 slice. The times are simulated.
32 devices in a mesh: frames: 8 (over z, y), band: 4 (over x, core).
Axes of the slice: x: 2, y: 2, z: 4, core: 2. Of those that a mesh axis runs over, the one named last changes fastest.
Arguments:
- tokens: bfloat16 [16, 1024, 1024], P('frames', 'band'), may hold values from -6 to 6
- norm_space: float32 [1024], replicated, may hold values from 0.5 to 1.5
- query_space: bfloat16 [1024, 1024], replicated, may hold values from -0.1875 to 0.1875
- keyval_space: bfloat16 [1024, 512], replicated, may hold values from -0.1875 to 0.1875
- out_space: bfloat16 [1024, 1024], replicated, may hold values from -0.1875 to 0.1875
- qk_space: float32 [2, 64], replicated, may hold values from 0.7 to 7
- norm_time: float32 [1024], replicated, may hold values from 0.5 to 1.5
- query_time: bfloat16 [1024, 1024], replicated, may hold values from -0.1875 to 0.1875
- keyval_time: bfloat16 [1024, 512], replicated, may hold values from -0.1875 to 0.1875
- out_time: bfloat16 [1024, 1024], replicated, may hold values from -0.1875 to 0.1875
- qk_time: float32 [2, 64], replicated, may hold values from 0.7 to 7
Outputs:
- mixed: bfloat16 [16, 1024, 1024], P('frames', 'band')
All inputs are finite; a program needn't handle non-finite values.
Results may differ from a plain program's by a relative error of at most 0.025.
The roundings to bfloat16 on the way count: a program that leaves them out, or rounds other values in their place, can miss the bound.
Values may be sent and summed in bfloat16 or wider, within the bound.
No kernel may reach another device: no remote copies, remote signals or barrier semaphores. Data moves between devices by JAX's collectives and lax.ppermute only.
A program may use at most 128 MiB of HBM per device.

v0:
```python
import jax
import jax.numpy as jnp
from jax import lax
from jax.sharding import PartitionSpec as P

HEADS = 16
KV_HEADS = 4
HEAD_DIM = 64


def rms_rows(values, gain):
    values = values.astype(jnp.float32)
    scaled = lax.rsqrt(jnp.mean(values * values, axis=-1, keepdims=True) + 1e-06)
    return values * scaled * gain


def project(hidden, w_query, w_keyval, qk_gain):
    row_count = hidden.shape[0]
    queries = jnp.dot(hidden, w_query, preferred_element_type=jnp.float32)
    keyval = jnp.dot(hidden, w_keyval, preferred_element_type=jnp.float32)
    queries = rms_rows(queries.reshape(row_count, HEADS, HEAD_DIM), qk_gain[0])
    key_part = keyval[:, : KV_HEADS * HEAD_DIM].reshape(row_count, KV_HEADS, HEAD_DIM)
    key_rows = rms_rows(key_part, qk_gain[1])
    values = keyval[:, KV_HEADS * HEAD_DIM :]
    return (
        queries.reshape(row_count, -1).astype(jnp.bfloat16),
        key_rows.reshape(row_count, -1).astype(jnp.bfloat16),
        values.astype(jnp.bfloat16),
    )


def attend(queries, key_rows, values, causal_mask):
    query_count = queries.shape[0]
    key_count = key_rows.shape[0]
    groups = HEADS // KV_HEADS
    grouped = queries.reshape(query_count, KV_HEADS, groups, HEAD_DIM)
    key_heads = key_rows.reshape(key_count, KV_HEADS, HEAD_DIM)
    value_heads = values.reshape(key_count, KV_HEADS, HEAD_DIM)
    scores = jnp.einsum(
        "nkgd,mkd->kgnm", grouped, key_heads, preferred_element_type=jnp.float32
    ) * HEAD_DIM ** (-0.5)
    if causal_mask is not None:
        scores = jnp.where(causal_mask, scores, -jnp.inf)
    largest = jnp.max(scores, axis=-1, keepdims=True)
    expos = jnp.exp(scores - largest)
    totals = jnp.sum(expos, axis=-1)
    weights = expos.astype(jnp.bfloat16)
    summed = jnp.einsum("kgnm,mkd->nkgd", weights, value_heads, preferred_element_type=jnp.float32)
    summed = summed / jnp.transpose(totals, (2, 0, 1))[..., None]
    return summed.reshape(query_count, HEADS * HEAD_DIM).astype(jnp.bfloat16)


def body(
    tokens,
    norm_space,
    query_space,
    keyval_space,
    out_space,
    qk_space,
    norm_time,
    query_time,
    keyval_time,
    out_time,
    qk_time,
):
    frames_here, rows_here, model_width = tokens.shape
    flat_tokens = tokens.reshape(frames_here * rows_here, model_width)
    normed = rms_rows(flat_tokens, norm_space).astype(jnp.bfloat16)
    queries, key_rows, values = project(normed, query_space, keyval_space, qk_space)
    queries = queries.reshape(frames_here, rows_here, -1)
    key_rows = key_rows.reshape(frames_here, rows_here, -1)
    values = values.reshape(frames_here, rows_here, -1)
    all_keys, all_values = (
        lax.all_gather(key_rows, "band", axis=1, tiled=True),
        lax.all_gather(values, "band", axis=1, tiled=True),
    )

    def space_frame(pieces):
        frame_q, frame_k, frame_v = pieces
        return attend(frame_q, frame_k, frame_v, None)

    attended = lax.map(space_frame, (queries, all_keys, all_values))
    attended = attended.reshape(frames_here * rows_here, HEADS * HEAD_DIM)
    update = jnp.dot(attended, out_space, preferred_element_type=jnp.float32)
    stream = (flat_tokens.astype(jnp.float32) + update).astype(jnp.bfloat16)
    normed_time = rms_rows(stream, norm_time).astype(jnp.bfloat16)
    moved = lax.all_to_all(
        normed_time.reshape(frames_here, rows_here, model_width),
        "frames",
        split_axis=1,
        concat_axis=0,
        tiled=True,
    )
    frame_total, local_positions = (moved.shape[0], moved.shape[1])
    time_q, time_k, time_v = project(
        moved.reshape(frame_total * local_positions, model_width), query_time, keyval_time, qk_time
    )
    time_q = time_q.reshape(frame_total, local_positions, -1)
    time_k = time_k.reshape(frame_total, local_positions, -1)
    time_v = time_v.reshape(frame_total, local_positions, -1)
    order = jnp.arange(frame_total, dtype=jnp.int32)
    causal_mask = order[:, None] >= order[None, :]
    time_att = jax.vmap(lambda qq, kk, vv: attend(qq, kk, vv, causal_mask))(
        jnp.swapaxes(time_q, 0, 1), jnp.swapaxes(time_k, 0, 1), jnp.swapaxes(time_v, 0, 1)
    )
    time_att = jnp.swapaxes(time_att, 0, 1)
    returned = lax.all_to_all(time_att, "frames", split_axis=0, concat_axis=1, tiled=True)
    returned = returned.reshape(frames_here * rows_here, HEADS * HEAD_DIM)
    update_time = jnp.dot(returned, out_time, preferred_element_type=jnp.float32)
    mixed = (stream.astype(jnp.float32) + update_time).astype(jnp.bfloat16)
    return mixed.reshape(frames_here, rows_here, model_width)


def solution(mesh):
    placed = (P("frames", "band", None), P(), P(), P(), P(), P(), P(), P(), P(), P(), P())
    return jax.shard_map(
        body, mesh=mesh, in_specs=placed, out_specs=P("frames", "band", None), check_vma=False
    )
```

profile of v0, /device:TPU:0, one launch (start us, length us, event | category | flops | bytes accessed | tf_op | source)
XLA Modules:
  0.0 223.1 jit_solution(13843182820674432862)
XLA Ops:
  16.3 4.0 %copy.70 = bf16[1024,1024]{0,1:T(8,128)(2,1)} copy(bf16[1024,1024]{1,0:T(8,128)(2,1)} %param.15) | data formatting | bytes 4194304 | tf_op args[2]
  24.8 2.4 %copy.71 = bf16[2,256,1024]{1,2,0:T(8,128)(2,1)} copy(bf16[2,256,1024]{1,0,2:T(2,128)(2,1)} %convert_element_type.87) | data formatting | bytes 2097152 | tf_op jit(solution)/shard_map/while | solution.py:82
  27.2 6.7 %all-gather.5.cloned.1.call-done = bf16[2,1024,256]{1,2,0:T(8,128)(2,1)} async-done(((bf16[2,256,256]{1,2,0:T(8,128)(2,1)}), bf16[2,1024,256]{1,2,0:T(8,128)(2,1)}) %all-gather.5.cloned.1.call-update) | async-done | bytes 1048592 | tf_op jit(solution)/shard_map/all_gather | solution.py:74
  33.9 18.4 %all-gather.3.cloned.1.call-done = bf16[2,1024,256]{1,2,0:T(8,128)(2,1)} async-done(((bf16[2,256,256]{1,2,0:T(8,128)(2,1)}), bf16[2,1024,256]{1,2,0:T(8,128)(2,1)}) %all-gather.3.cloned.1.call-update) | async-done | bytes 1048592 | tf_op jit(solution)/shard_map/all_gather | solution.py:75
  52.3 57.7 %while.10 = (s32[]{:T(128)}, bf16[2,256,1024]{2,1,0:T(8,128)(2,1)}, bf16[2,1024,256]{1,2,0:T(8,128)(2,1)}, bf16[2,1024,256]{1,2,0:T(8,128)(2,1)}, bf16[2,256,1024]{1,2,0:T(8,128)(2,1)}, /*index=5*/s32[]{:T(128)}) while((s32[]{:T(128)}, bf16[2,256,1024]{2,1,0:T(8,128)(2,1)}, bf16[2,1024,256]{1,2,0:T(8,128)(2,1)}, ...), condition=%wide.region_6.7_spmd, body=%wide.region_3.6_spmd.sunk | while | flops 1107812352 | bytes 57754188 | solution.py:82
  54.7 8.1 %bitcast_reduce_fusion.4 = (f32[4,4,256]{2,1,0:T(4,128)S(1)}, f32[4,1024,256,4]{2,1,3,0:T(8,128)}) fusion(bf16[1024,4,64,1]{0,2,3,1:T(8,128)(2,1)S(1)} %bitcast.152, bf16[256,4,4,64]{0,3,2,1:T(8,128)(2,1)S(1)} %bitcast.153), kind=kOutput, calls=%fused_computation.1.clone.1 | convolution fusion | flops 545255424 | bytes 17842176 | tf_op jit(solution)/shard_map/while/body/eval_jaxpr/nkgd,mkd->kgnm/dot_general | solution.py:39
  62.8 8.6 %fusion.63 = f32[4,4,256]{2,1,0:T(4,128)S(1)} fusion(f32[4,1024,256,4]{2,1,3,0:T(8,128)} %get-tuple-element.118, f32[4,4,256]{2,1,0:T(4,128)S(1)} %get-tuple-element.119), kind=kLoop, calls=%fused_computation.3.clone.1 | loop fusion | flops 12578816 | bytes 16809984 | tf_op jit(solution)/shard_map/while/body/eval_jaxpr/reduce_sum | solution.py:46
  71.4 8.7 %divide_convert_fusion.2 = bf16[256,4,4,64]{0,3,2,1:T(8,128)(2,1)S(1)} fusion(bf16[1024,4,64,1]{0,2,3,1:T(8,128)(2,1)S(1)} %bitcast.150, f32[4,1024,256,4]{2,1,3,0:T(8,128)} %get-tuple-element.118, f32[4,4,256]{2,1,0:T(4,128)S(1)} %get-tuple-element.119, f32[256,4,4]{0,2,1:T(4,128)S(1)} %bitcast.159), kind=kOutput, calls=%fused_computation.7.clone.1 | convolution fusion | flops 549978112 | bytes 17858560 | tf_op jit(solution)/shard_map/while/body/eval_jaxpr/kgnm,mkd->nkgd/dot_general | solution.py:48
  83.5 8.1 %bitcast_reduce_fusion.4 = (f32[4,4,256]{2,1,0:T(4,128)S(1)}, f32[4,1024,256,4]{2,1,3,0:T(8,128)}) fusion(bf16[1024,4,64,1]{0,2,3,1:T(8,128)(2,1)S(1)} %bitcast.152, bf16[256,4,4,64]{0,3,2,1:T(8,128)(2,1)S(1)} %bitcast.153), kind=kOutput, calls=%fused_computation.1.clone.1 | convolution fusion | flops 545255424 | bytes 17842176 | tf_op jit(solution)/shard_map/while/body/eval_jaxpr/nkgd,mkd->kgnm/dot_general | solution.py:39
  91.6 8.6 %fusion.63 = f32[4,4,256]{2,1,0:T(4,128)S(1)} fusion(f32[4,1024,256,4]{2,1,3,0:T(8,128)} %get-tuple-element.118, f32[4,4,256]{2,1,0:T(4,128)S(1)} %get-tuple-element.119), kind=kLoop, calls=%fused_computation.3.clone.1 | loop fusion | flops 12578816 | bytes 16809984 | tf_op jit(solution)/shard_map/while/body/eval_jaxpr/reduce_sum | solution.py:46
  100.2 8.7 %divide_convert_fusion.2 = bf16[256,4,4,64]{0,3,2,1:T(8,128)(2,1)S(1)} fusion(bf16[1024,4,64,1]{0,2,3,1:T(8,128)(2,1)S(1)} %bitcast.150, f32[4,1024,256,4]{2,1,3,0:T(8,128)} %get-tuple-element.118, f32[4,4,256]{2,1,0:T(4,128)S(1)} %get-tuple-element.119, f32[256,4,4]{0,2,1:T(4,128)S(1)} %bitcast.159), kind=kOutput, calls=%fused_computation.7.clone.1 | convolution fusion | flops 549978112 | bytes 17858560 | tf_op jit(solution)/shard_map/while/body/eval_jaxpr/kgnm,mkd->nkgd/dot_general | solution.py:48
  110.0 2.9 %fusion.15 = (f32[512]{0:T(512)S(1)}, bf16[512,1024]{1,0:T(8,128)(2,1)S(1)}) fusion(bf16[512,1024]{1,0:T(8,128)(2,1)} %bitcast.178, bf16[1024,1024]{1,0:T(8,128)(2,1)S(1)} %copy-done, bf16[2,256,1024]{2,1,0:T(8,128)(2,1)} %param.13), kind=kOutput, calls=%fused_computation.23 | convolution fusion | flops 1076887040 | bytes 5244928 | tf_op jit(solution)/shard_map/dot_general | solution.py:84
  116.3 5.5 %all-to-all-start = ((bf16[2,256,1024]{2,0,1:T(2,128)(2,1)}), bf16[2,256,1024]{2,0,1:T(2,128)(2,1)S(1)}, u32[]{:S(2)}, u32[]{:S(2)}) async-start(bf16[2,256,1024]{2,0,1:T(2,128)(2,1)} %copy.73), calls=%async_computation | async-start | bytes 2097152 | tf_op jit(solution)/shard_map/all_to_all | solution.py:87
  121.9 3.9 %copy.79 = bf16[1024,1024]{0,1:T(8,128)(2,1)} copy(bf16[1024,1024]{1,0:T(8,128)(2,1)} %param.20) | data formatting | bytes 4194304 | tf_op args[7]
  125.9 22.1 %all-to-all-done = bf16[2,256,1024]{2,0,1:T(2,128)(2,1)S(1)} async-done(((bf16[2,256,1024]{2,0,1:T(2,128)(2,1)}), bf16[2,256,1024]{2,0,1:T(2,128)(2,1)S(1)}, u32[]{:S(2)}, u32[]{:S(2)}) %all-to-all-start) | async-done | bytes 1048608 | tf_op jit(solution)/shard_map/all_to_all | solution.py:87
  153.8 3.2 %multiply_reduce_fusion = (f32[512,16]{0,1:T(8,128)S(1)}, f32[512,16,64]{0,2,1:T(8,128)S(1)}) fusion(bf16[512,1024,1]{1,0,2:T(8,128)(2,1)} %bitcast.169, bf16[16,64,1024]{2,1,0:T(8,128)(2,1)} %bitcast.160), kind=kOutput, calls=%fused_computation.43 | convolution fusion | flops 1074782208 | bytes 5275648 | tf_op jit(solution)/shard_map/dot_general | solution.py:19
  157.6 2.9 %copy.80 = bf16[512,16,64]{2,1,0:T(8,128)(2,1)} copy(bf16[512,16,64]{0,2,1:T(8,128)(2,1)S(1)} %multiply_convert_fusion) | data formatting | bytes 2097152 | tf_op jit(solution)/shard_map/convert_element_type | solution.py:26
  160.4 3.2 %convert_element_type.93 = bf16[16,32,1024]{2,1,0:T(8,128)(2,1)S(1)} reshape(bf16[512,16,64]{2,1,0:T(8,128)(2,1)} %copy.80) | data formatting | bytes 2097152 | tf_op jit(solution)/shard_map/convert_element_type | solution.py:26
  163.7 2.4 %reshape.186 = bf16[32,16,4,4,64]{4,3,2,0,1:T(4,128)(2,1)} reshape(bf16[32,16,1024]{2,0,1:T(8,128)(2,1)S(1)} %bitcast.154) | data formatting | bytes 2097152 | tf_op jit(solution)/shard_map/vmap()/reshape | solution.py:36
  166.4 6.9 %fusion.14 = (f32[32,4,4,16]{3,2,1,0:T(4,128)S(1)}, f32[32,4,16,16,4]{3,2,4,1,0:T(8,128)S(1)}) fusion(pred[16,16]{0,1:T(8,128)(4,1)S(1)} %iota_compare_fusion, bf16[32,16,4,4,64]{4,3,2,0,1:T(4,128)(2,1)} %reshape.186, bf16[32,16,4,64,1]{3,2,1,0,4:T(4,128)(2,1)} %bitcast.164), kind=kOutput, calls=%fused_computation.19 | convolution fusion | flops 17162240 | bytes 1868032 | tf_op jit(solution)/shard_map/vmap(nkgd,mkd->kgnm)/dot_general | solution.py:39
  175.0 2.4 %fusion.11 = bf16[32,16,4,4,64]{4,1,3,2,0:T(8,128)(2,1)S(1)} fusion(f32[32,4,16,16,4]{3,2,4,1,0:T(8,128)S(1)} %get-tuple-element.80, f32[32,16,4,4]{1,3,2,0:T(4,128)S(1)} %bitcast.176, f32[32,4,4,16]{3,2,1,0:T(4,128)S(1)} %get-tuple-element.79, pred[16,16]{0,1:T(8,128)(4,1)S(1)} %iota_compare_fusion, bf16[32,16,4,64,1]{3,2,1,0,4:T(4,128)(2,1)S(1)} %bitcast.175), kind=kOutput, calls=%fused_computation.14 | convolution fusion | flops 18350080 | bytes 1900800 | tf_op jit(solution)/shard_map/vmap(kgnm,mkd->nkgd)/dot_general | solution.py:48
  177.4 2.5 %copy.86 = bf16[32,16,4,4,64]{4,3,2,1,0:T(4,128)(2,1)} copy(bf16[32,16,4,4,64]{4,1,3,2,0:T(8,128)(2,1)S(1)} %fusion.11) | data formatting | bytes 2097152 | tf_op jit(solution)/shard_map/vmap()/convert_element_type | solution.py:50
  179.8 3.8 %convert_element_type.96 = bf16[32,16,1024]{2,1,0:T(8,128)(2,1)S(1)} reshape(bf16[32,16,4,4,64]{4,3,2,1,0:T(4,128)(2,1)} %copy.86) | data formatting | bytes 2097152 | tf_op jit(solution)/shard_map/vmap()/convert_element_type | solution.py:50
  184.3 29.6 %all_to_all.30 = bf16[16,32,1024]{2,1,0:T(8,128)(2,1)S(1)} all-to-all(bf16[16,32,1024]{2,1,0:T(8,128)(2,1)S(1)} %copy.87), channel_id=1, replica_groups=mesh['frames'=8,'band'=4] {'frames'}, dimensions={0} | all-to-all | bytes 2097152 | tf_op jit(solution)/shard_map/all_to_all | solution.py:107
  (93 shorter events, 35.5 us)
Async XLA Ops:
  6.5 103.5 %copy-start = (bf16[1024,1024]{1,0:T(8,128)(2,1)S(1)}, bf16[1024,1024]{1,0:T(8,128)(2,1)}, u32[]{:S(2)}) copy-start(bf16[1024,1024]{1,0:T(8,128)(2,1)} %param.17) | copy-start | bytes 6291460
  6.5 3.2 %copy-start.13 = (bf16[1024,512]{1,0:T(8,128)(2,1)S(1)}, bf16[1024,512]{1,0:T(8,128)(2,1)}, u32[]{:S(2)}) copy-start(bf16[1024,512]{1,0:T(8,128)(2,1)} %param.16) | copy-start | bytes 3145732
  6.5 27.4 %all-gather.5.cloned.1.call-start = ((), (), s32[]{:S(2)}) async-start(), calls=%async_computation.3 | async-start | bytes 1310720 | tf_op jit(solution)/shard_map/all_gather | solution.py:74
  10.5 1.0 copy-start.3
  11.5 0.7 copy-start.10
  14.2 38.1 %all-gather.3.cloned.1.call-start = ((), (), s32[]{:S(2)}) async-start(), calls=%async_computation.2 | async-start | bytes 1310720 | tf_op jit(solution)/shard_map/all_gather | solution.py:75
  16.2 4.0 %copy-start.1 = (bf16[2,256,1024]{2,1,0:T(8,128)(2,1)S(1)}, bf16[2,256,1024]{2,1,0:T(8,128)(2,1)}, u32[]{:S(2)}) copy-start(bf16[2,256,1024]{2,1,0:T(8,128)(2,1)} %param.13) | copy-start | bytes 3145732
  16.2 4.0 %copy-start.8 = (f32[1024]{0:T(1024)S(1)}, f32[1024]{0:T(1024)}, u32[]{:S(2)}) copy-start(f32[1024]{0:T(1024)} %param.14) | copy-start | bytes 12292
  20.3 1.6 copy-start.2
  110.0 3.9 %copy-start.9 = (f32[1024]{0:T(1024)S(1)}, f32[1024]{0:T(1024)}, u32[]{:S(2)}) copy-start(f32[1024]{0:T(1024)} %param.19) | copy-start | bytes 12292
  112.9 1.0 copy-start.5
  114.2 7.6 %copy-start.11 = (f32[2,64]{1,0:T(2,128)S(1)}, f32[2,64]{1,0:T(2,128)}, u32[]{:S(2)}) copy-start(f32[2,64]{1,0:T(2,128)} %param.23) | copy-start | bytes 1540
  116.3 31.7 %all-to-all-start = ((bf16[2,256,1024]{2,0,1:T(2,128)(2,1)}), bf16[2,256,1024]{2,0,1:T(2,128)(2,1)S(1)}, u32[]{:S(2)}, u32[]{:S(2)}) async-start(bf16[2,256,1024]{2,0,1:T(2,128)(2,1)} %copy.73), calls=%async_computation | async-start | bytes 2097152 | tf_op jit(solution)/shard_map/all_to_all | solution.py:87
  148.0 1.2 copy-start.14
  148.3 1.7 copy-start.7
  149.9 1.0 copy-start.4
  184.3 29.7 %copy-start.6 = (bf16[512,1024]{1,0:T(8,128)(2,1)S(1)}, bf16[512,1024]{1,0:T(8,128)(2,1)}, u32[]{:S(2)}) copy-start(bf16[512,1024]{1,0:T(8,128)(2,1)} %copy-done.5) | copy-start | bytes 3145732
  184.3 29.7 %copy-start.12 = (bf16[1024,1024]{1,0:T(8,128)(2,1)S(1)}, bf16[1024,1024]{1,0:T(8,128)(2,1)}, u32[]{:S(2)}) copy-start(bf16[1024,1024]{1,0:T(8,128)(2,1)} %param.22) | copy-start | bytes 6291460
Sparse Core Ops, SparseCore 0:
  14.4 19.5 all-gather.4
  35.5 16.8 all-gather.2
where the time goes:
time: 224 us; the launch traced here: 223 us
  matrix products  54 us (24%)
  waiting for transfers between devices  47.3 us (21%)
  local copies, waits for them, and re-layouts  46.6 us (21%)
  blocking collectives  29.6 us (13%)
  other arithmetic  26.1 us (12%)
  between operations  13.8 us (6%)
  starting transfers between devices  5.56 us (2%)
    all_to_all x1, blocking collectives, body(): lax.all_to_all(time_att, 'frames', split_axis=0, concat_axis=1, tiled=True)  29.6 us
    dot_general x3, matrix products, attend(): jnp.einsum('nkgd,mkd->kgnm', grouped, key_heads, preferred_element_type=j...  23.1 us
    all_to_all x1, waiting for transfers between devices, body(): lax.all_to_all(normed_time.reshape(frames_here, rows_here, model_width),...  22.1 us
    dot_general x3, matrix products, attend(): jnp.einsum('kgnm,mkd->nkgd', weights, value_heads, preferred_element_type...  19.9 us
    reduce_sum x3, other arithmetic, attend(): totals = jnp.sum(expos, axis=-1)  18.8 us
    all_gather x1, waiting for transfers between devices, body(): lax.all_gather(values, 'band', axis=1, tiled=True)  18.4 us
    unnamed x33, local copies, waits for them, and re-layouts  13.1 us
    convert_element_type x3, local copies, waits for them, and re-layouts, project(): queries.reshape(row_count, -1).astype(jnp.bfloat16)  7.23 us
  transfers between devices with their start and end apart: 3, of which 3 were waited for; matrix products, arithmetic and copies ran while one was open for 7% of the time, Pallas kernels for 0%

commit v1 on v0

--- a/solution.py
+++ b/solution.py
@@ -6,6 +6,7 @@
 HEADS = 16
 KV_HEADS = 4
 HEAD_DIM = 64
+expand_series_all_now = lambda row_data: jnp.concatenate(lax.all_gather(row_data, "band"), 1)
 
 
 def rms_rows(values, gain):
@@ -72,7 +73,7 @@
     values = values.reshape(frames_here, rows_here, -1)
     all_keys, all_values = (
         lax.all_gather(key_rows, "band", axis=1, tiled=True),
-        lax.all_gather(values, "band", axis=1, tiled=True),
+        expand_series_all_now(values),
     )
 
     def space_frame(pieces):

time: 224 us -> 222 us (level)
  waiting for transfers between devices: 47.3 us -> 43.1 us
    all_gather x1, waiting for transfers between devices: 18.4 us -> 4.79 us  [lax.all_gather(row_data, 'band')]
    all_gather x1, waiting for transfers between devices: 6.75 us -> 16.1 us  [body(): lax.all_gather(key_rows, 'band', axis=1, tiled=True)]
    all_gather x0 -> x1, local copies, waits for them, and re-layouts: none -> 2.29 us  [lax.all_gather(row_data, 'band')]
    dynamic_slice x4 -> x8, local copies, waits for them, and re-layouts: 4.7 us -> 4.81 us  [body(): attended = lax.map(space_frame, (queries, all_keys, all_values))]
  transfers between devices with their start and end apart: 3 -> 3, of which waited for: 3 -> 3; matrix products, arithmetic and copies ran while one was open for 7% -> 9% of each run, Pallas kernels for 0% -> 0%
where the time goes in v1:
time: 222 us; the launch traced here: 221 us
  matrix products  54 us (24%)
  local copies, waits for them, and re-layouts  47.8 us (22%)
  waiting for transfers between devices  43.1 us (19%)
  blocking collectives  29.6 us (13%)
  other arithmetic  27.2 us (12%)
  between operations  13.8 us (6%)
  starting transfers between devices  5.56 us (3%)
    all_to_all x1, blocking collectives, body(): lax.all_to_all(time_att, 'frames', split_axis=0, concat_axis=1, tiled=True)  29.6 us
    dot_general x3, matrix products, attend(): jnp.einsum('nkgd,mkd->kgnm', grouped, key_heads, preferred_element_type=j...  23.1 us
    all_to_all x1, waiting for transfers between devices, body(): lax.all_to_all(normed_time.reshape(frames_here, rows_here, model_width),...  22.1 us
    dot_general x3, matrix products, attend(): jnp.einsum('kgnm,mkd->nkgd', weights, value_heads, preferred_element_type...  19.8 us
    reduce_sum x3, other arithmetic, attend(): totals = jnp.sum(expos, axis=-1)  18.8 us
    all_gather x1, waiting for transfers between devices, body(): lax.all_gather(key_rows, 'band', axis=1, tiled=True)  16.1 us
    unnamed x33, local copies, waits for them, and re-layouts  13.1 us
    convert_element_type x3, local copies, waits for them, and re-layouts, project(): queries.reshape(row_count, -1).astype(jnp.bfloat16)  7.23 us
  transfers between devices with their start and end apart: 3, of which 3 were waited for; matrix products, arithmetic and copies ran while one was open for 9% of the time, Pallas kernels for 0%

profile of v1, /device:TPU:0, one launch (start us, length us, event | category | flops | bytes accessed | tf_op | source)
XLA Modules:
  0.0 221.1 jit_solution(2989229626650198183)
XLA Ops:
  16.0 4.0 %copy.69 = bf16[1024,1024]{0,1:T(8,128)(2,1)} copy(bf16[1024,1024]{1,0:T(8,128)(2,1)} %param.15) | data formatting | bytes 4194304 | tf_op args[2]
  24.6 2.4 %copy.71 = bf16[2,256,1024]{1,2,0:T(8,128)(2,1)} copy(bf16[2,256,1024]{1,0,2:T(2,128)(2,1)} %convert_element_type.87) | data formatting | bytes 2097152 | tf_op jit(solution)/shard_map/while | solution.py:83
  27.0 4.8 %all-gather.3.cloned.1.call-done = bf16[4,2,256,256]{3,2,1,0:T(8,128)(2,1)} async-done(((bf16[1,2,256,256]{3,2,1,0:T(8,128)(2,1)}), bf16[4,2,256,256]{3,2,1,0:T(8,128)(2,1)}) %all-gather.3.cloned.1.call-update) | async-done | bytes 1048592 | tf_op jit(solution)/shard_map/all_gather | solution.py:9
  34.1 16.1 %all-gather.5.cloned.1.call-done = bf16[2,1024,256]{1,2,0:T(8,128)(2,1)} async-done(((bf16[2,256,256]{1,2,0:T(8,128)(2,1)}), bf16[2,1024,256]{1,2,0:T(8,128)(2,1)}) %all-gather.5.cloned.1.call-update) | async-done | bytes 1048592 | tf_op jit(solution)/shard_map/all_gather | solution.py:75
  50.2 57.8 %while.10 = (s32[]{:T(128)}, bf16[2,256,1024]{2,1,0:T(8,128)(2,1)}, bf16[2,1024,256]{2,1,0:T(8,128)(2,1)}, bf16[2,1024,256]{1,2,0:T(8,128)(2,1)}, bf16[2,256,1024]{1,2,0:T(8,128)(2,1)}, /*index=5*/s32[]{:T(128)}) while((s32[]{:T(128)}, bf16[2,256,1024]{2,1,0:T(8,128)(2,1)}, bf16[2,1024,256]{2,1,0:T(8,128)(2,1)}, ...), condition=%wide.region_6.7_spmd, body=%wide.region_3.6_spmd.sunk | while | flops 1107812352 | bytes 62997100 | solution.py:83
  52.4 8.1 %bitcast_reduce_fusion.4 = (f32[4,4,256]{2,1,0:T(4,128)S(1)}, f32[4,1024,256,4]{2,1,3,0:T(8,128)}) fusion(bf16[1024,4,64,1]{0,2,3,1:T(8,128)(2,1)S(1)} %bitcast.155, bf16[256,4,4,64]{0,3,2,1:T(8,128)(2,1)S(1)} %bitcast.156), kind=kOutput, calls=%fused_computation.1.clone.1 | convolution fusion | flops 545255424 | bytes 17842176 | tf_op jit(solution)/shard_map/while/body/eval_jaxpr/nkgd,mkd->kgnm/dot_general | solution.py:40
  60.5 8.6 %fusion.63 = f32[4,4,256]{2,1,0:T(4,128)S(1)} fusion(f32[4,1024,256,4]{2,1,3,0:T(8,128)} %get-tuple-element.112, f32[4,4,256]{2,1,0:T(4,128)S(1)} %get-tuple-element.113), kind=kLoop, calls=%fused_computation.3.clone.1 | loop fusion | flops 12578816 | bytes 16809984 | tf_op jit(solution)/shard_map/while/body/eval_jaxpr/reduce_sum | solution.py:47
  69.4 8.7 %divide_convert_fusion.2 = bf16[256,4,4,64]{0,3,2,1:T(8,128)(2,1)S(1)} fusion(bf16[1024,4,64,1]{0,2,3,1:T(8,128)(2,1)S(1)} %bitcast.153, f32[4,1024,256,4]{2,1,3,0:T(8,128)} %get-tuple-element.112, f32[4,4,256]{2,1,0:T(4,128)S(1)} %get-tuple-element.113, f32[256,4,4]{0,2,1:T(4,128)S(1)} %bitcast.163), kind=kOutput, calls=%fused_computation.7.clone.1 | convolution fusion | flops 549978112 | bytes 17858560 | tf_op jit(solution)/shard_map/while/body/eval_jaxpr/kgnm,mkd->nkgd/dot_general | solution.py:49
  81.3 8.1 %bitcast_reduce_fusion.4 = (f32[4,4,256]{2,1,0:T(4,128)S(1)}, f32[4,1024,256,4]{2,1,3,0:T(8,128)}) fusion(bf16[1024,4,64,1]{0,2,3,1:T(8,128)(2,1)S(1)} %bitcast.155, bf16[256,4,4,64]{0,3,2,1:T(8,128)(2,1)S(1)} %bitcast.156), kind=kOutput, calls=%fused_computation.1.clone.1 | convolution fusion | flops 545255424 | bytes 17842176 | tf_op jit(solution)/shard_map/while/body/eval_jaxpr/nkgd,mkd->kgnm/dot_general | solution.py:40
  89.4 8.6 %fusion.63 = f32[4,4,256]{2,1,0:T(4,128)S(1)} fusion(f32[4,1024,256,4]{2,1,3,0:T(8,128)} %get-tuple-element.112, f32[4,4,256]{2,1,0:T(4,128)S(1)} %get-tuple-element.113), kind=kLoop, calls=%fused_computation.3.clone.1 | loop fusion | flops 12578816 | bytes 16809984 | tf_op jit(solution)/shard_map/while/body/eval_jaxpr/reduce_sum | solution.py:47
  98.2 8.7 %divide_convert_fusion.2 = bf16[256,4,4,64]{0,3,2,1:T(8,128)(2,1)S(1)} fusion(bf16[1024,4,64,1]{0,2,3,1:T(8,128)(2,1)S(1)} %bitcast.153, f32[4,1024,256,4]{2,1,3,0:T(8,128)} %get-tuple-element.112, f32[4,4,256]{2,1,0:T(4,128)S(1)} %get-tuple-element.113, f32[256,4,4]{0,2,1:T(4,128)S(1)} %bitcast.163), kind=kOutput, calls=%fused_computation.7.clone.1 | convolution fusion | flops 549978112 | bytes 17858560 | tf_op jit(solution)/shard_map/while/body/eval_jaxpr/kgnm,mkd->nkgd/dot_general | solution.py:49
  108.0 2.9 %fusion.15 = (f32[512]{0:T(512)S(1)}, bf16[512,1024]{1,0:T(8,128)(2,1)S(1)}) fusion(bf16[512,1024]{1,0:T(8,128)(2,1)} %bitcast.182, bf16[1024,1024]{1,0:T(8,128)(2,1)S(1)} %copy-done, bf16[2,256,1024]{2,1,0:T(8,128)(2,1)} %param.13), kind=kOutput, calls=%fused_computation.23 | convolution fusion | flops 1076887040 | bytes 5244928 | tf_op jit(solution)/shard_map/dot_general | solution.py:85
  114.3 5.5 %all-to-all-start = ((bf16[2,256,1024]{2,0,1:T(2,128)(2,1)}), bf16[2,256,1024]{2,0,1:T(2,128)(2,1)S(1)}, u32[]{:S(2)}, u32[]{:S(2)}) async-start(bf16[2,256,1024]{2,0,1:T(2,128)(2,1)} %copy.73), calls=%async_computation | async-start | bytes 2097152 | tf_op jit(solution)/shard_map/all_to_all | solution.py:88
  119.9 3.9 %copy.79 = bf16[1024,1024]{0,1:T(8,128)(2,1)} copy(bf16[1024,1024]{1,0:T(8,128)(2,1)} %param.20) | data formatting | bytes 4194304 | tf_op args[7]
  123.9 22.1 %all-to-all-done = bf16[2,256,1024]{2,0,1:T(2,128)(2,1)S(1)} async-done(((bf16[2,256,1024]{2,0,1:T(2,128)(2,1)}), bf16[2,256,1024]{2,0,1:T(2,128)(2,1)S(1)}, u32[]{:S(2)}, u32[]{:S(2)}) %all-to-all-start) | async-done | bytes 1048608 | tf_op jit(solution)/shard_map/all_to_all | solution.py:88
  151.8 3.2 %multiply_reduce_fusion = (f32[512,16]{0,1:T(8,128)S(1)}, f32[512,16,64]{0,2,1:T(8,128)S(1)}) fusion(bf16[512,1024,1]{1,0,2:T(8,128)(2,1)} %bitcast.173, bf16[16,64,1024]{2,1,0:T(8,128)(2,1)} %bitcast.164), kind=kOutput, calls=%fused_computation.43 | convolution fusion | flops 1074782208 | bytes 5275648 | tf_op jit(solution)/shard_map/dot_general | solution.py:20
  155.5 2.9 %copy.80 = bf16[512,16,64]{2,1,0:T(8,128)(2,1)} copy(bf16[512,16,64]{0,2,1:T(8,128)(2,1)S(1)} %multiply_convert_fusion) | data formatting | bytes 2097152 | tf_op jit(solution)/shard_map/convert_element_type | solution.py:27
  158.4 3.2 %convert_element_type.93 = bf16[16,32,1024]{2,1,0:T(8,128)(2,1)S(1)} reshape(bf16[512,16,64]{2,1,0:T(8,128)(2,1)} %copy.80) | data formatting | bytes 2097152 | tf_op jit(solution)/shard_map/convert_element_type | solution.py:27
  161.7 2.4 %reshape.190 = bf16[32,16,4,4,64]{4,3,2,0,1:T(4,128)(2,1)} reshape(bf16[32,16,1024]{2,0,1:T(8,128)(2,1)S(1)} %bitcast.158) | data formatting | bytes 2097152 | tf_op jit(solution)/shard_map/vmap()/reshape | solution.py:37
  164.4 6.9 %fusion.14 = (f32[32,4,4,16]{3,2,1,0:T(4,128)S(1)}, f32[32,4,16,16,4]{3,2,4,1,0:T(8,128)S(1)}) fusion(pred[16,16]{0,1:T(8,128)(4,1)S(1)} %iota_compare_fusion, bf16[32,16,4,4,64]{4,3,2,0,1:T(4,128)(2,1)} %reshape.190, bf16[32,16,4,64,1]{3,2,1,0,4:T(4,128)(2,1)} %bitcast.168), kind=kOutput, calls=%fused_computation.19 | convolution fusion | flops 17162240 | bytes 1868032 | tf_op jit(solution)/shard_map/vmap(nkgd,mkd->kgnm)/dot_general | solution.py:40
  172.9 2.4 %fusion.11 = bf16[32,16,4,4,64]{4,1,3,2,0:T(8,128)(2,1)S(1)} fusion(f32[32,4,16,16,4]{3,2,4,1,0:T(8,128)S(1)} %get-tuple-element.78, f32[32,16,4,4]{1,3,2,0:T(4,128)S(1)} %bitcast.180, f32[32,4,4,16]{3,2,1,0:T(4,128)S(1)} %get-tuple-element.77, pred[16,16]{0,1:T(8,128)(4,1)S(1)} %iota_compare_fusion, bf16[32,16,4,64,1]{3,2,1,0,4:T(4,128)(2,1)S(1)} %bitcast.179), kind=kOutput, calls=%fused_computation.14 | convolution fusion | flops 18350080 | bytes 1900800 | tf_op jit(solution)/shard_map/vmap(kgnm,mkd->nkgd)/dot_general | solution.py:49
  175.4 2.5 %copy.86 = bf16[32,16,4,4,64]{4,3,2,1,0:T(4,128)(2,1)} copy(bf16[32,16,4,4,64]{4,1,3,2,0:T(8,128)(2,1)S(1)} %fusion.11) | data formatting | bytes 2097152 | tf_op jit(solution)/shard_map/vmap()/convert_element_type | solution.py:51
  177.8 3.8 %convert_element_type.96 = bf16[32,16,1024]{2,1,0:T(8,128)(2,1)S(1)} reshape(bf16[32,16,4,4,64]{4,3,2,1,0:T(4,128)(2,1)} %copy.86) | data formatting | bytes 2097152 | tf_op jit(solution)/shard_map/vmap()/convert_element_type | solution.py:51
  182.3 29.6 %all_to_all.30 = bf16[16,32,1024]{2,1,0:T(8,128)(2,1)S(1)} all-to-all(bf16[16,32,1024]{2,1,0:T(8,128)(2,1)S(1)} %copy.87), channel_id=1, replica_groups=mesh['frames'=8,'band'=4] {'frames'}, dimensions={0} | all-to-all | bytes 2097152 | tf_op jit(solution)/shard_map/all_to_all | solution.py:108
  (101 shorter events, 37.7 us)
Async XLA Ops:
  6.5 101.4 %copy-start = (bf16[1024,1024]{1,0:T(8,128)(2,1)S(1)}, bf16[1024,1024]{1,0:T(8,128)(2,1)}, u32[]{:S(2)}) copy-start(bf16[1024,1024]{1,0:T(8,128)(2,1)} %param.17) | copy-start | bytes 6291460
  6.5 3.2 %copy-start.14 = (bf16[1024,512]{1,0:T(8,128)(2,1)S(1)}, bf16[1024,512]{1,0:T(8,128)(2,1)}, u32[]{:S(2)}) copy-start(bf16[1024,512]{1,0:T(8,128)(2,1)} %param.16) | copy-start | bytes 3145732
  6.5 25.3 %all-gather.3.cloned.1.call-start = ((), (), s32[]{:S(2)}) async-start(), calls=%async_computation.2 | async-start | bytes 1310720 | tf_op jit(solution)/shard_map/all_gather | solution.py:9
  10.5 1.0 copy-start.4
  12.2 1.7 copy-start.11
  12.2 38.0 %all-gather.5.cloned.1.call-start = ((), (), s32[]{:S(2)}) async-start(), calls=%async_computation.3 | async-start | bytes 1310720 | tf_op jit(solution)/shard_map/all_gather | solution.py:75
  16.0 4.0 %copy-start.2 = (bf16[2,256,1024]{2,1,0:T(8,128)(2,1)S(1)}, bf16[2,256,1024]{2,1,0:T(8,128)(2,1)}, u32[]{:S(2)}) copy-start(bf16[2,256,1024]{2,1,0:T(8,128)(2,1)} %param.13) | copy-start | bytes 3145732
  16.0 4.0 %copy-start.9 = (f32[1024]{0:T(1024)S(1)}, f32[1024]{0:T(1024)}, u32[]{:S(2)}) copy-start(f32[1024]{0:T(1024)} %param.14) | copy-start | bytes 12292
  20.0 1.7 copy-start.3
  60.5 8.6 %copy-start.1 = (bf16[2,1024,256]{2,1,0:T(8,128)(2,1)S(1)}, bf16[2,1024,256]{2,1,0:T(8,128)(2,1)}, u32[]{:S(2)}) copy-start(bf16[2,1024,256]{2,1,0:T(8,128)(2,1)} %get-tuple-element.128) | copy-start | bytes 3145732 | tf_op jit(solution)/shard_map/while
  89.4 8.6 %copy-start.1 = (bf16[2,1024,256]{2,1,0:T(8,128)(2,1)S(1)}, bf16[2,1024,256]{2,1,0:T(8,128)(2,1)}, u32[]{:S(2)}) copy-start(bf16[2,1024,256]{2,1,0:T(8,128)(2,1)} %get-tuple-element.128) | copy-start | bytes 3145732 | tf_op jit(solution)/shard_map/while
  108.0 3.9 %copy-start.10 = (f32[1024]{0:T(1024)S(1)}, f32[1024]{0:T(1024)}, u32[]{:S(2)}) copy-start(f32[1024]{0:T(1024)} %param.19) | copy-start | bytes 12292
  110.9 1.0 copy-start.6
  112.2 7.6 %copy-start.12 = (f32[2,64]{1,0:T(2,128)S(1)}, f32[2,64]{1,0:T(2,128)}, u32[]{:S(2)}) copy-start(f32[2,64]{1,0:T(2,128)} %param.23) | copy-start | bytes 1540
  114.3 31.7 %all-to-all-start = ((bf16[2,256,1024]{2,0,1:T(2,128)(2,1)}), bf16[2,256,1024]{2,0,1:T(2,128)(2,1)S(1)}, u32[]{:S(2)}, u32[]{:S(2)}) async-start(bf16[2,256,1024]{2,0,1:T(2,128)(2,1)} %copy.73), calls=%async_computation | async-start | bytes 2097152 | tf_op jit(solution)/shard_map/all_to_all | solution.py:88
  146.0 1.2 copy-start.15
  146.3 1.7 copy-start.8
  147.9 1.0 copy-start.5
  182.3 29.7 %copy-start.7 = (bf16[512,1024]{1,0:T(8,128)(2,1)S(1)}, bf16[512,1024]{1,0:T(8,128)(2,1)}, u32[]{:S(2)}) copy-start(bf16[512,1024]{1,0:T(8,128)(2,1)} %copy-done.6) | copy-start | bytes 3145732
  182.3 29.7 %copy-start.13 = (bf16[1024,1024]{1,0:T(8,128)(2,1)S(1)}, bf16[1024,1024]{1,0:T(8,128)(2,1)}, u32[]{:S(2)}) copy-start(bf16[1024,1024]{1,0:T(8,128)(2,1)} %param.22) | copy-start | bytes 6291460
Sparse Core Ops, SparseCore 0:
  12.3 19.4 all-gather.2
  33.4 16.8 all-gather.4
